TPU v7x, 256 devices: a whole 4x4x8 slice. The times are simulated.
256 devices in a mesh: dp: 16 (over z_hi, x, core), fsdp: 16 (over z_lo, y).
Axes of the slice: x: 4, y: 4, z: 8 (z_hi: 2, z_lo: 4; z = z_hi * 4 + z_lo), core: 2. Of those that a mesh axis runs over, the one named last changes fastest.
Arguments:
- attn_heads: bfloat16 [512, 4096], P('dp', 'fsdp'), may hold values from -6 to 6
- out_proj: bfloat16 [4096, 4608], P('fsdp'), may hold values from -0.09375 to 0.09375
- resid_pre: bfloat16 [512, 4608], P(('dp', 'fsdp')), may hold values from -25 to 25
- post_gain: float32 [4608], replicated, may hold values from 0.5 to 1.5
- enc_weight: bfloat16 [4608, 65536], P(None, ('dp', 'fsdp')), may hold values from -0.09375 to 0.09375
- enc_bias: float32 [65536], P(('dp', 'fsdp')), may hold values from -3 to 3
- dec_weight: bfloat16 [65536, 4608], P(('dp', 'fsdp')), may hold values from -0.046875 to 0.046875
- dec_bias: float32 [4608], replicated, may hold values from -3 to 3
Outputs:
- enc_grad: bfloat16 [4608, 65536], P(None, ('dp', 'fsdp'))
- enc_bias_grad: float32 [65536], P(('dp', 'fsdp'))
- dec_grad: bfloat16 [65536, 4608], P(('dp', 'fsdp'))
- dec_bias_grad: float32 [4608], replicated
- loss: float32 [], replicated
All inputs are finite; a program needn't handle non-finite values.
Results may differ from a plain program's by a relative error of at most 0.013.
Values may be sent and summed in bfloat16 or wider, within the bound.
A program may use at most 128 MiB of HBM per device.

v0:
```python
import jax
import jax.numpy as jnp
from jax import lax
from jax.sharding import PartitionSpec as P

SPARSITY = 0.25
SMOOTHING = 0.1
EPSILON = 1e-06


def finish(summed, resid_rows, post_gain):
    scale = lax.rsqrt(jnp.mean(summed * summed, axis=-1, keepdims=True) + EPSILON)
    return (resid_rows.astype(jnp.float32) + summed * scale * post_gain).astype(jnp.bfloat16)


def body(attn_heads, out_proj, resid_pre, post_gain, enc_weight, enc_bias, dec_weight, dec_bias):
    block = attn_heads
    summed = lax.psum_scatter(
        jnp.dot(block, out_proj, preferred_element_type=jnp.float32),
        "fsdp",
        scatter_dimension=0,
        tiled=True,
    )
    resid_own = finish(summed, resid_pre, post_gain)
    resid_all = lax.all_gather(resid_own, ("dp", "fsdp"), axis=0, tiled=True)
    preact = jnp.dot(resid_all, enc_weight, preferred_element_type=jnp.float32) + enc_bias
    latents = jnp.maximum(preact, 0.0)
    latents_b = latents.astype(jnp.bfloat16)
    row_norms = jnp.sqrt(jnp.sum(jnp.square(dec_weight.astype(jnp.float32)), axis=1) + EPSILON)
    penalty_local = jnp.sum(latents * row_norms)
    penalty_total = lax.psum(penalty_local, ("dp", "fsdp"))
    block = latents_b
    recon = lax.psum_scatter(
        jnp.dot(block, dec_weight, preferred_element_type=jnp.float32),
        ("dp", "fsdp"),
        scatter_dimension=0,
        tiled=True,
    )
    recon = recon + dec_bias
    error = recon - resid_own.astype(jnp.float32)
    error_local = jnp.sum(error * error)
    error_total = lax.psum(error_local, ("dp", "fsdp"))
    loss = (0.5 * error_total + SPARSITY * penalty_total) / (
        resid_all.shape[0] * resid_all.shape[1]
    )
    error_b = error.astype(jnp.bfloat16)
    error_all = lax.all_gather(error_b, ("dp", "fsdp"), axis=0, tiled=True)
    dec_bias_grad = jnp.sum(error_all, axis=0, dtype=jnp.float32)
    usage = jnp.sum(latents, axis=0)
    dec_grad = lax.dot_general(
        latents_b, error_all, (((0,), (0,)), ((), ())), preferred_element_type=jnp.float32
    )
    dec_grad = (
        dec_grad + SPARSITY * (usage / row_norms)[:, None] * dec_weight.astype(jnp.float32)
    ).astype(jnp.bfloat16)
    latent_grad = lax.dot_general(
        error_all, dec_weight, (((1,), (1,)), ((), ())), preferred_element_type=jnp.float32
    )
    latent_grad = latent_grad + SPARSITY * row_norms
    preact_grad = latent_grad * jax.nn.sigmoid(preact / SMOOTHING)
    enc_bias_grad = jnp.sum(preact_grad, axis=0)
    enc_grad = lax.dot_general(
        resid_all,
        preact_grad.astype(jnp.bfloat16),
        (((0,), (0,)), ((), ())),
        preferred_element_type=jnp.float32,
    ).astype(jnp.bfloat16)
    return (enc_grad, enc_bias_grad, dec_grad, dec_bias_grad, loss)


def solution(mesh):
    placed = (
        P("dp", "fsdp"),
        P("fsdp", None),
        P(("dp", "fsdp"), None),
        P(),
        P(None, ("dp", "fsdp")),
        P(("dp", "fsdp")),
        P(("dp", "fsdp"), None),
        P(),
    )
    return jax.shard_map(
        body,
        mesh=mesh,
        in_specs=placed,
        out_specs=(P(None, ("dp", "fsdp")), P(("dp", "fsdp")), P(("dp", "fsdp"), None), P(), P()),
        check_vma=False,
    )
```

profile of v0, /device:TPU:99, one launch (start us, length us, event | category | flops | bytes accessed | tf_op | source)
XLA Modules:
  0.0 1927.3 jit_solution(9511033964533940527)
XLA Ops:
  7.2 0.0 copy-start
  7.2 0.0 all-reduce.6.cloned.1.call-start
  7.2 1.6 copy-done
  8.8 2.0 fusion.9
  10.9 0.0 all-reduce.6.cloned.1.call-update
  10.9 0.0 all-gather.5.cloned.1.call-start
  11.0 1.3 dynamic-slice
  12.9 144.5 %all-reduce.6.cloned.1.call-done = f32[32,4608]{1,0:T(8,128)} async-done(((f32[32,4608]{1,0:T(8,128)}), f32[32,4608]{1,0:T(8,128)}) %all-reduce.6.cloned.1.call-update) | async-done | bytes 589840
  157.3 1.1 multiply_reduce_fusion.2
  158.4 1.6 add_convert_fusion
  160.0 0.0 all-gather.5.cloned.1.call-update
  160.1 0.0 all-reduce.8.cloned.1.call-start
  160.1 2.2 fusion.1
  162.3 0.0 copy-start.6
  162.3 727.9 %all-gather.5.cloned.1.call-done = bf16[256,2,4608]{2,1,0:T(2,128)(2,1)} async-done(((bf16[1,2,4608]{2,1,0:T(2,128)(2,1)}), bf16[256,2,4608]{2,1,0:T(2,128)(2,1)}) %all-gather.5.cloned.1.call-update) | async-done | bytes 4718608 | tf_op jit(solution)/shard_map/all_gather | solution.py:25
  890.2 7.6 reshape.38
  897.8 0.0 copy-done.6
  897.8 0.0 copy-start.2
  897.8 5.2 multiply_reduce_fusion
  903.0 0.0 copy-done.2
  903.0 5.1 fusion.4
  908.1 0.0 copy-start.4
  908.1 0.0 copy-start.5
  908.1 0.0 all-reduce.8.cloned.1.call-update
  908.1 0.0 all-gather.7.cloned.1.call-start
  908.1 275.0 %all-reduce.8.cloned.1.call-done = f32[512,4608]{1,0:T(8,128)} async-done(((f32[512,4608]{1,0:T(8,128)}), f32[512,4608]{1,0:T(8,128)}) %all-reduce.8.cloned.1.call-update) | async-done | bytes 9437200
  1183.1 0.0 copy-done.4
  1183.1 0.0 copy-done.5
  1183.1 2.2 multiply_reduce_fusion.1
  1185.3 0.0 all-gather.7.cloned.1.call-update
  1185.3 72.2 %all-reduce.2 = (f32[]{:T(128)}, f32[]{:T(128)}) all-reduce(f32[]{:T(128)} %get-tuple-element.9, f32[]{:T(128)} %get-tuple-element.5), channel_id=1, replica_groups=mesh['dp'=16,'fsdp'=16] {'dp','fsdp'}, use_global_device_ids=true, to_apply=%region_8.0 | all-reduce | flops 2 | bytes 16 | tf_op jit(solution)/shard_map/psum | solution.py:42
  1258.8 639.6 %all-gather.7.cloned.1.call-done = bf16[256,2,4608]{2,1,0:T(2,128)(2,1)} async-done(((bf16[1,2,4608]{2,1,0:T(2,128)(2,1)}), bf16[256,2,4608]{2,1,0:T(2,128)(2,1)}) %all-gather.7.cloned.1.call-update) | async-done | bytes 4718608 | tf_op jit(solution)/shard_map/all_gather | solution.py:47
  1898.4 7.6 reshape.40
  1906.0 0.0 copy-start.1
  1906.0 0.0 slice-start
  1906.0 4.1 convert_reduce_fusion
  1910.1 0.0 copy-done.1
  1910.1 0.0 copy-start.3
  1910.1 0.0 slice-start.1
  1910.1 3.8 fusion.8
  1913.9 0.0 copy-done.3
  1913.9 2.9 fusion
  1916.7 0.0 slice-done
  1916.7 0.0 slice-done.1
  1916.8 2.9 convolution_convert_fusion
  (4 shorter events, 0.0 us)
Async XLA Ops:
  7.2 1.7 copy-start
  7.2 150.2 %all-reduce.6.cloned.1.call-start = ((), (), s32[]{:S(2)}) async-start(), calls=%async_computation.2 | async-start | bytes 1179648
  10.9 879.3 %all-gather.5.cloned.1.call-start = ((), (), s32[]{:S(2)}) async-start(), calls=%async_computation | async-start | bytes 4737024 | tf_op jit(solution)/shard_map/all_gather | solution.py:25
  160.1 1023.0 %all-reduce.8.cloned.1.call-start = ((), (), s32[]{:S(2)}) async-start(), calls=%async_computation.3 | async-start | bytes 18874368
  162.3 735.4 %copy-start.6 = (f32[256]{0:T(256)S(1)}, f32[256]{0:T(256)}, u32[]{:S(2)}) copy-start(f32[256]{0:T(256)} %param.13) | copy-start | bytes 3076
  897.8 5.2 copy-start.2
  908.1 275.0 %copy-start.4 = (bf16[2,4608]{1,0:T(2,128)(2,1)S(1)}, bf16[2,4608]{1,0:T(2,128)(2,1)}, u32[]{:S(2)}) copy-start(bf16[2,4608]{1,0:T(2,128)(2,1)} %add_convert_fusion) | copy-start | bytes 55300
  908.1 275.0 %copy-start.5 = (f32[4608]{0:T(1024)S(1)}, f32[4608]{0:T(1024)}, u32[]{:S(2)}) copy-start(f32[4608]{0:T(1024)} %param.15) | copy-start | bytes 55300
  908.1 990.3 %all-gather.7.cloned.1.call-start = ((), (), s32[]{:S(2)}) async-start(), calls=%async_computation.1 | async-start | bytes 4737024 | tf_op jit(solution)/shard_map/all_gather | solution.py:47
  1906.0 4.1 copy-start.1
  1906.0 10.7 slice-start
  1910.1 3.8 copy-start.3
  1910.1 6.7 slice-start.1
Sparse Core Ops, SparseCore 0:
  11.2 146.0 all-reduce.5
  160.2 729.9 all-gather.4
  908.2 274.8 all-reduce.7
  1185.4 712.9 all-gather.6
where the time goes:
time: 1930 us
  waiting for transfers between devices  1790 us (93%)
  blocking collectives  72.2 us (4%)
  matrix products  21.9 us (1%)
    all_gather x1, waiting for transfers between devices, body(): resid_all = lax.all_gather(resid_own, ('dp', 'fsdp'), axis=0, tiled=True)  728 us
    all_gather x1, waiting for transfers between devices, body(): error_all = lax.all_gather(error_b, ('dp', 'fsdp'), axis=0, tiled=True)  640 us
    unnamed x6, waiting for transfers between devices  419 us
    psum x1, blocking collectives, body(): error_total = lax.psum(error_local, ('dp', 'fsdp'))  72.2 us
  transfers between devices with their start and end apart: 4, of which 4 were waited for; matrix products, arithmetic and copies ran while one was open for 0% of the time, Pallas kernels for 0%

commit v1 on v0

--- a/solution.py
+++ b/solution.py
@@ -44,7 +44,10 @@
         resid_all.shape[0] * resid_all.shape[1]
     )
     error_b = error.astype(jnp.bfloat16)
-    error_all = lax.all_gather(error_b, ("dp", "fsdp"), axis=0, tiled=True)
+    size = lax.axis_size(("dp", "fsdp"))
+    blocks = jnp.stack([error_b for _ in range(size)])
+    blocks = lax.all_to_all(blocks, ("dp", "fsdp"), split_axis=0, concat_axis=0)
+    error_all = jnp.concatenate(blocks, axis=0)
     dec_bias_grad = jnp.sum(error_all, axis=0, dtype=jnp.float32)
     usage = jnp.sum(latents, axis=0)
     dec_grad = lax.dot_general(

time: 1930 us -> 1380 us (0.72)
  waiting for transfers between devices: 1790 us -> 1150 us
  blocking collectives: 72.2 us -> 146 us
    all_gather x1 -> x0, waiting for transfers between devices: 640 us -> none  [body(): error_all = lax.all_gather(error_b, ('dp', 'fsdp'), axis=0, tiled=True)]
    psum x1, blocking collectives: 72.2 us -> 146 us  [body(): error_total = lax.psum(error_local, ('dp', 'fsdp'))]
    unnamed x6 -> x5, waiting for transfers between devices: 419 us -> 419 us
  transfers between devices with their start and end apart: 4 -> 4, of which waited for: 4 -> 3; matrix products, arithmetic and copies ran while one was open for 0% -> 0% of each run, Pallas kernels for 0% -> 0%
where the time goes in v1:
time: 1380 us
  waiting for transfers between devices  1150 us (83%)
  blocking collectives  146 us (11%)
  matrix products  23.3 us (2%)
  local copies, waits for them, and re-layouts  22.7 us (2%)
  between operations  16.9 us (1%)
    all_gather x1, waiting for transfers between devices, body(): resid_all = lax.all_gather(resid_own, ('dp', 'fsdp'), axis=0, tiled=True)  728 us
    unnamed x5, waiting for transfers between devices  419 us
    psum x1, blocking collectives, body(): error_total = lax.psum(error_local, ('dp', 'fsdp'))  146 us
  transfers between devices with their start and end apart: 4, of which 3 were waited for; matrix products, arithmetic and copies ran while one was open for 0% of the time, Pallas kernels for 0%

profile of v1, /device:TPU:99, one launch (start us, length us, event | category | flops | bytes accessed | tf_op | source)
XLA Modules:
  0.0 1377.8 jit_solution(3137325471463486131)
XLA Ops:
  7.2 0.0 copy-start
  7.2 0.0 all-reduce.6.cloned.1.call-start
  7.2 1.6 copy-done
  8.8 2.0 fusion.10
  10.9 0.0 all-reduce.6.cloned.1.call-update
  10.9 0.0 all-gather.3.cloned.1.call-start
  11.0 1.3 dynamic-slice
  12.9 144.5 %all-reduce.6.cloned.1.call-done = f32[32,4608]{1,0:T(8,128)} async-done(((f32[32,4608]{1,0:T(8,128)}), f32[32,4608]{1,0:T(8,128)}) %all-reduce.6.cloned.1.call-update) | async-done | bytes 589840
  157.3 1.1 multiply_reduce_fusion.2
  158.4 1.6 add_convert_fusion
  160.0 0.0 all-gather.3.cloned.1.call-update
  160.1 0.0 all-reduce.8.cloned.1.call-start
  160.1 2.2 fusion.1
  162.3 0.0 copy-start.6
  162.3 727.9 %all-gather.3.cloned.1.call-done = bf16[256,2,4608]{2,1,0:T(2,128)(2,1)} async-done(((bf16[1,2,4608]{2,1,0:T(2,128)(2,1)}), bf16[256,2,4608]{2,1,0:T(2,128)(2,1)}) %all-gather.3.cloned.1.call-update) | async-done | bytes 4718608 | tf_op jit(solution)/shard_map/all_gather | solution.py:25
  890.2 7.6 reshape.44
  897.8 0.0 copy-done.6
  897.8 0.0 copy-start.1
  897.8 5.2 multiply_reduce_fusion
  903.0 0.0 copy-done.1
  903.0 5.1 fusion.4
  908.1 0.0 copy-start.4
  908.1 0.0 copy-start.5
  908.1 0.0 all-reduce.8.cloned.1.call-update
  908.1 274.9 %all-reduce.8.cloned.1.call-done = f32[512,4608]{1,0:T(8,128)} async-done(((f32[512,4608]{1,0:T(8,128)}), f32[512,4608]{1,0:T(8,128)}) %all-reduce.8.cloned.1.call-update) | async-done | bytes 9437200
  1183.0 0.0 copy-done.4
  1183.0 0.0 copy-done.5
  1183.0 1.6 multiply_reduce_fusion.1
  1184.6 4.6 stack.2
  1189.2 11.2 all-to-all-start
  1200.4 146.5 %all-reduce.2 = (f32[]{:T(128)}, f32[]{:T(128)}) all-reduce(f32[]{:T(128)} %get-tuple-element.9, f32[]{:T(128)} %get-tuple-element.5), channel_id=1, replica_groups=mesh['dp'=16,'fsdp'=16] {'dp','fsdp'}, use_global_device_ids=true, to_apply=%region_8.0 | all-reduce | flops 2 | bytes 16 | tf_op jit(solution)/shard_map/psum | solution.py:42
  1348.2 0.0 all-to-all-done
  1348.2 0.0 slice-start
  1348.2 7.7 reshape.42
  1355.9 0.0 copy-start.2
  1355.9 0.0 copy-start.3
  1355.9 0.0 slice-start.1
  1355.9 5.2 fusion.9
  1361.1 0.0 copy-done.2
  1361.1 0.0 copy-done.3
  1361.1 2.9 fusion
  1364.0 0.0 slice-done
  1364.0 0.0 slice-done.1
  1364.0 2.9 convolution_convert_fusion
  1366.8 3.3 convert_reduce_fusion
  (4 shorter events, 0.0 us)
Async XLA Ops:
  7.2 1.7 copy-start
  7.2 150.2 %all-reduce.6.cloned.1.call-start = ((), (), s32[]{:S(2)}) async-start(), calls=%async_computation.2 | async-start | bytes 1179648
  10.9 879.3 %all-gather.3.cloned.1.call-start = ((), (), s32[]{:S(2)}) async-start(), calls=%async_computation.1 | async-start | bytes 4737024 | tf_op jit(solution)/shard_map/all_gather | solution.py:25
  160.1 1023.0 %all-reduce.8.cloned.1.call-start = ((), (), s32[]{:S(2)}) async-start(), calls=%async_computation.3 | async-start | bytes 18874368
  162.3 735.4 %copy-start.6 = (f32[256]{0:T(256)S(1)}, f32[256]{0:T(256)}, u32[]{:S(2)}) copy-start(f32[256]{0:T(256)} %param.13) | copy-start | bytes 3076
  897.8 5.2 copy-start.1
  908.1 275.0 %copy-start.4 = (bf16[2,4608]{1,0:T(2,128)(2,1)S(1)}, bf16[2,4608]{1,0:T(2,128)(2,1)}, u32[]{:S(2)}) copy-start(bf16[2,4608]{1,0:T(2,128)(2,1)} %add_convert_fusion) | copy-start | bytes 55300
  908.1 275.0 %copy-start.5 = (f32[4608]{0:T(1024)S(1)}, f32[4608]{0:T(1024)}, u32[]{:S(2)}) copy-start(f32[4608]{0:T(1024)} %param.15) | copy-start | bytes 55300
  1189.2 159.0 %all-to-all-start = ((bf16[256,2,4608]{2,1,0:T(2,128)(2,1)}), bf16[256,2,4608]{2,1,0:T(2,128)(2,1)}, u32[]{:S(2)}, u32[]{:S(2)}) async-start(bf16[256,2,4608]{2,1,0:T(2,128)(2,1)} %stack.2), calls=%async_computation | async-start | bytes 9437184 | tf_op jit(solution)/shard_map/all_to_all | solution.py:49
  1348.2 15.8 %slice-start = ((s8[4718592]{0:T(1024)(128)(4,1)}), s8[524288]{0:T(1024)(128)(4,1)S(1)}, s32[]{:S(2)}) async-start(s8[4718592]{0:T(1024)(128)(4,1)} %bitcast.12), calls=%async_computation.4 | async-start | bytes 1048576
  1355.9 5.2 copy-start.2
  1355.9 5.2 copy-start.3
  1355.9 8.1 slice-start.1
Sparse Core Ops, SparseCore 0:
  11.2 146.0 all-reduce.5
  160.2 729.9 all-gather.2
  908.2 274.7 all-reduce.7
